TPU v7x, 32 devices: a whole 2x2x4 slice. The times are simulated.
32 devices in a mesh: row: 4 (over y, core), col: 8 (over z, x).
Axes of the slice: x: 2, y: 2, z: 4, core: 2. Of those that a mesh axis runs over, the one named last changes fastest.
Arguments:
- amplitudes: float32 [16, 16, 768, 768], P('row', 'col'), may hold values from -0.6 to 0.6
- integrals: float32 [16, 16, 768, 768], P('row', 'col'), may hold values from -6 to 6
- factors: float32 [16, 2048, 768], P('col', 'row'), may hold values from -0.21 to 0.21
- occ_energy: float32 [16], replicated, may hold values from -2 to -0.5
- vir_energy: float32 [768], replicated, may hold values from 0.5 to 3
Outputs:
- new_amplitudes: float32 [16, 16, 768, 768], P('row', 'col')
All inputs are finite; a program needn't handle non-finite values.
Results may differ from a plain program's by a relative error of at most 0.00005.
Values sent between devices are 32-bit elements; how exact they have to be, the bound alone decides.
A program may use at most 192 MiB of HBM per device.

v0:
```python
import functools

import jax
import jax.numpy as jnp
from jax import lax
from jax.experimental import pallas as pl
from jax.experimental.pallas import tpu as pltpu
from jax.sharding import PartitionSpec as P


VMEM_LIMIT = 63 * 1024 * 1024
NN = (((1,), (0,)), ((), ()))
NT = (((1,), (1,)), ((), ()))
TN = (((0,), (0,)), ((), ()))


def split(x):
    hi = x.astype(jnp.bfloat16)
    return hi, (x - hi.astype(jnp.float32)).astype(jnp.bfloat16)


def dot3(lhs, rhs, dims):
    mul = functools.partial(lax.dot_general, dimension_numbers=dims, preferred_element_type=jnp.float32)
    return mul(lhs[0], rhs[0]) + (mul(lhs[0], rhs[1]) + mul(lhs[1], rhs[0]))


def left_kernel(tile, oj, vir, t_ref, l_ref, x_ref, hi_ref, lo_ref):
    @pl.when(pl.program_id(1) == 0)
    def _():
        for j in range(oj):
            hi, lo = split(t_ref[0, j])
            hi_ref[:, j * vir:(j + 1) * vir] = hi
            lo_ref[:, j * vir:(j + 1) * vir] = lo

    @pl.loop(0, x_ref.shape[0] // tile)
    def _(step):
        rows = pl.ds(step * tile, tile)
        x_ref[rows, :] = dot3(split(l_ref[rows, :]), (hi_ref[...], lo_ref[...]), NT)


def left_product(amplitudes, factors, part, parts):
    oi, oj, vir, _ = amplitudes.shape
    aux = factors.shape[0]
    block = min(512, aux)
    own = oi // parts
    return pl.pallas_call(
        functools.partial(left_kernel, min(256, block), oj, vir),
        grid=(own, aux // block),
        in_specs=[
            pl.BlockSpec((1, oj, vir, vir), lambda i, p: (part * own + i, 0, 0, 0)),
            pl.BlockSpec((block, oj * vir), lambda i, p: (p, 0)),
        ],
        out_specs=pl.BlockSpec((block, vir), lambda i, p: (p, i)),
        out_shape=jax.ShapeDtypeStruct((aux, own * vir), jnp.float32),
        scratch_shapes=[pltpu.VMEM((vir, oj * vir), jnp.bfloat16)] * 2,
        compiler_params=pltpu.CompilerParams(vmem_limit_bytes=VMEM_LIMIT),
        cost_estimate=pl.CostEstimate(flops=6 * own * oj * vir * vir * aux, bytes_accessed=4 * (own * oj * vir * vir + aux * own * (oj + 1) * vir), transcendentals=0),
        name="left_product",
    )(amplitudes, factors)


def right_kernel(oi, vir, parts, t_ref, *refs):
    l_refs, (y_ref, hi_ref, lo_ref) = refs[:parts], refs[parts:]

    @pl.when(pl.program_id(1) == 0)
    def _():
        for i in range(oi):
            hi, lo = split(t_ref[i, 0])
            hi_ref[i * vir:(i + 1) * vir, :] = hi
            lo_ref[i * vir:(i + 1) * vir, :] = lo

    total = 0.0
    for part, l_ref in enumerate(l_refs):
        wide = l_ref.shape[1]
        rows = slice(part * wide, (part + 1) * wide)
        total = total + dot3(split(l_ref[...]), (hi_ref[rows, :], lo_ref[rows, :]), NN)
    y_ref[...] = total


def right_product(amplitudes, factors, rows, piece, pieces):
    oi, oj, vir, _ = amplitudes.shape
    aux = factors[0].shape[0]
    block = aux // (rows * pieces)
    parts = len(factors)
    wide = factors[0].shape[1]
    return pl.pallas_call(
        functools.partial(right_kernel, oi, vir, parts),
        grid=(oj, rows),
        in_specs=[pl.BlockSpec((oi, 1, vir, vir), lambda j, p: (0, j, 0, 0))]
        + [pl.BlockSpec((block, wide), lambda j, p: (p * pieces + piece, 0))] * parts,
        out_specs=pl.BlockSpec((block, vir), lambda j, p: (p, j)),
        out_shape=jax.ShapeDtypeStruct((rows * block, oj * vir), jnp.float32),
        scratch_shapes=[pltpu.VMEM((oi * vir, vir), jnp.bfloat16)] * 2,
        compiler_params=pltpu.CompilerParams(vmem_limit_bytes=VMEM_LIMIT),
        cost_estimate=pl.CostEstimate(flops=6 * oi * oj * vir * vir * rows * block, bytes_accessed=4 * (oi * oj * vir * vir + rows * block * oj * (oi + 1) * vir), transcendentals=0),
        name="right_product",
    )(amplitudes, *factors)


def base_kernel(k_ref, lr_ref, sc_ref, *refs):
    out_ref = refs[-1]
    step = pl.program_id(2)
    term = dot3(split(lr_ref[...]), split(sc_ref[...]), TN)

    @pl.when(step == 0)
    def _():
        out_ref[0, 0] = k_ref[0, 0] + term

    @pl.when(step > 0)
    def _():
        out_ref[0, 0] += term


def final_kernel(first, left_ref, right_ref, vir_row_ref, vir_col_ref, k_ref, sr_ref, lc_ref, *refs):
    out_ref, acc_ref = refs[-2:]
    i, j, step = pl.program_id(0), pl.program_id(1), pl.program_id(2)

    @pl.when(step == 0)
    def _():
        acc_ref[...] = k_ref[0, 0]

    acc_ref[...] += dot3(split(sr_ref[...]), split(lc_ref[...]), TN)

    @pl.when(step == pl.num_programs(2) - 1)
    def _():
        pair = left_ref[first + i] + right_ref[j]
        out_ref[0, 0] = acc_ref[...] / (pair - vir_col_ref[...] - vir_row_ref[...])


def tile_call(kernel, shape, aux, part, parts, block, lead, pair_in, row_in, col_in, earlier, in_place, scratch):
    oi, oj, vir, _ = shape
    own = oi // parts
    first = part * own
    pair = pl.BlockSpec((1, 1, vir, vir), lambda i, j, p: (first + i, j, 0, 0))
    args = [array for array, _ in lead] + [pair_in, row_in, col_in]
    specs = [spec for _, spec in lead] + [
        pair,
        pl.BlockSpec((block, vir), lambda i, j, p: (p, i)),
        pl.BlockSpec((block, vir), lambda i, j, p: (p, j)),
    ]
    alias = {len(lead): 0} if in_place else {}
    if earlier is not None:
        alias = {len(args): 0}
        args.append(earlier)
        specs.append(pl.BlockSpec(memory_space=pl.ANY))
    return pl.pallas_call(
        kernel,
        grid=(own, oj, aux // block),
        in_specs=specs,
        out_specs=pair,
        out_shape=jax.ShapeDtypeStruct(shape, jnp.float32),
        input_output_aliases=alias,
        scratch_shapes=scratch,
        compiler_params=pltpu.CompilerParams(vmem_limit_bytes=VMEM_LIMIT),
        cost_estimate=pl.CostEstimate(flops=6 * own * oj * vir * vir * aux, bytes_accessed=4 * own * oj * (2 * vir * vir + 2 * aux * vir), transcendentals=0),
    )(*args)


def base(integrals, fac_row, sum_col, part, parts, earlier):
    aux = fac_row.shape[0]
    return tile_call(base_kernel, integrals.shape, aux, part, parts, min(1024, aux), [], integrals, fac_row, sum_col, earlier, False, [])


def final(so_far, sum_row, fac_col, occ_left, occ_right, vir_energy, part, parts):
    oi, _, vir, _ = so_far.shape
    aux = sum_row.shape[0]
    smem = pl.BlockSpec(memory_space=pltpu.SMEM)
    lead = [
        (occ_left, smem),
        (occ_right, smem),
        (vir_energy[None, :], pl.BlockSpec((1, vir), lambda i, j, p: (0, 0))),
        (vir_energy[:, None], pl.BlockSpec((vir, 1), lambda i, j, p: (0, 0))),
    ]
    kernel = functools.partial(final_kernel, part * (oi // parts))
    return tile_call(kernel, so_far.shape, aux, part, parts, min(1024, aux), lead, so_far, sum_row, fac_col, None, True, [pltpu.VMEM((vir, vir), jnp.float32)])


def ring_of(cols):
    return list(range(0, cols, 2)) + list(range(1, cols, 2))[::-1]


def ring_facts(cols, way):
    ring = ring_of(cols)
    perm = [(ring[k], ring[(k + way) % cols]) for k in range(cols)]
    place = [ring.index(c) for c in range(cols)]
    at = jnp.asarray(place, jnp.int32)[lax.axis_index("col")]
    owner = lambda back: jnp.asarray(ring, jnp.int32)[lax.rem(at + cols - way * back + cols, cols)]
    return perm, owner


def ring_gather(shard, cols):
    half = shard.shape[0] // 2
    full = jnp.zeros((shard.shape[0] * cols, shard.shape[1]), shard.dtype)
    full = lax.dynamic_update_slice(full, shard, (lax.axis_index("col") * 2 * half, 0))
    ways = [(way, shard[k * half:(k + 1) * half], *ring_facts(cols, way)) for k, way in enumerate((1, -1))]
    held = [w[1] for w in ways]
    for step in range(1, cols):
        for k, (way, _, perm, owner) in enumerate(ways):
            held[k] = lax.ppermute(held[k], "col", perm)
        for k, (way, _, perm, owner) in enumerate(ways):
            full = lax.dynamic_update_slice(full, held[k], (owner(step) * 2 * half + k * half, 0))
    return full


def ring_scatter(array, cols):
    size = array.shape[0] // cols
    half = size // 2
    sums = []
    for k, way in enumerate((1, -1)):
        perm, owner = ring_facts(cols, way)
        mine = lambda back: lax.dynamic_slice(array, (owner(back) * size + k * half, 0), (half, array.shape[1]))
        held = mine(1)
        for step in range(1, cols):
            held = lax.ppermute(held, "col", perm)
            held = held + mine(step + 1)
        sums.append(held)
    return jnp.concatenate(sums, axis=0)


def pick(pieces, index):
    return lax.dynamic_index_in_dim(pieces, index, 0, keepdims=False)


def to_row(shard, rows, cols):
    ratio = cols // rows
    col = lax.axis_index("col")
    parts = shard.reshape(ratio, shard.shape[0] // ratio, shard.shape[1])
    got = []
    for k in range(ratio):
        perm = [
            (r * cols + c, (c // ratio) * cols + r * ratio + (c + k) % ratio)
            for r in range(rows) for c in range(cols)
        ]
        got.append(lax.ppermute(pick(parts, lax.rem(col + k, ratio)), ("row", "col"), perm))
    got = jnp.stack(got)
    return jnp.concatenate([pick(got, lax.rem(col + ratio - m, ratio)) for m in range(ratio)], axis=1)


def to_col(shard, rows, cols):
    ratio = cols // rows
    col = lax.axis_index("col")
    parts = jnp.stack(jnp.split(shard, ratio, axis=1))
    got = []
    for k in range(ratio):
        perm = [
            ((c // ratio) * cols + r * ratio + (c + k) % ratio, r * cols + c)
            for r in range(rows) for c in range(cols)
        ]
        got.append(lax.ppermute(pick(parts, lax.rem(col + ratio - k, ratio)), ("row", "col"), perm))
    got = jnp.stack(got)
    return jnp.concatenate([pick(got, lax.rem(m + ratio - lax.rem(col, ratio), ratio)) for m in range(ratio)], axis=0)


def shards(rows, cols, amplitudes, integrals, factors, occ_energy, vir_energy):
    oi, oj, vir, _ = amplitudes.shape
    parts = 2 if oi % 2 == 0 else 1
    pieces = 4
    wide = oi // parts * vir
    own = jnp.transpose(factors, (1, 0, 2)).reshape(factors.shape[1], oj * vir)
    fac_col = lax.all_gather(own, "row", axis=0, tiled=True)
    moved = to_row(own, rows, cols)
    fac_row = [ring_gather(moved[:, g * wide:(g + 1) * wide], cols) for g in range(parts)]
    left = []
    for g in range(parts):
        left.append(left_product(amplitudes, fac_col, g, parts))
    left = [ring_scatter(part, cols) for part in left]
    right = []
    for h in range(pieces):
        right.append(right_product(amplitudes, fac_row, rows, h, pieces))
    right = [lax.psum_scatter(piece, "row", scatter_dimension=0, tiled=True) for piece in right]
    right = to_row(jnp.concatenate(right, axis=0), rows, cols)
    summed = [2.0 * left[g] - right[:, g * wide:(g + 1) * wide] for g in range(parts)]
    sum_col = lax.all_gather(to_col(jnp.concatenate(summed, axis=1), rows, cols), "row", axis=0, tiled=True)
    sum_row = [ring_gather(part, cols) for part in summed]
    occ_left = lax.dynamic_slice_in_dim(occ_energy, lax.axis_index("row") * oi, oi)
    occ_right = lax.dynamic_slice_in_dim(occ_energy, lax.axis_index("col") * oj, oj)
    out = None
    for g in range(parts):
        out = base(integrals, fac_row[g], sum_col, g, parts, out)
    for g in range(parts):
        out = final(out, sum_row[g], fac_col, occ_left, occ_right, vir_energy, g, parts)
    return out


def solution(mesh):
    cols = mesh.shape["col"]
    return jax.shard_map(
        functools.partial(shards, mesh.shape["row"], cols),
        mesh=mesh,
        in_specs=(
            P("row", "col", None, None),
            P("row", "col", None, None),
            P("col", "row", None),
            P(),
            P(),
        ),
        out_specs=P("row", "col", None, None),
        check_vma=False,
    )
```

profile of v0, /device:TPU:0, one launch (start us, length us, event | category | flops | bytes accessed | tf_op | source)
XLA Modules:
  0.0 1504.6 jit_solution(7662133297556886495)
XLA Ops:
  28.3 50.1 %collective-permute-done.1 = f32[256,1536]{1,0:T(8,128)S(1)} collective-permute-done((f32[256,1536]{1,0:T(8,128)}, f32[256,1536]{1,0:T(8,128)S(1)}, u32[]{:S(2)}, u32[]{:S(2)}) %collective-permute-start.1) | collective-permute-done | bytes 1572896 | tf_op jit(solution)/shard_map/ppermute | solution.py:234
  81.9 14.4 collective-permute-start.2
  104.1 72.9 %collective-permute-start.30 = (f32[128,1536]{1,0:T(8,128)S(1)}, f32[128,1536]{1,0:T(8,128)S(1)}, u32[]{:S(2)}, u32[]{:S(2)}) collective-permute-start(f32[128,1536]{1,0:T(8,128)S(1)} %get-tuple-element.60), channel_id=1, source_target_pairs={{0,2},{2,4},{4,6},{6,7},{7,5},{5,3},{3,1},{1,0},{8,10},{10,12},{12... | collective-permute-start | bytes 2359304 | tf_op jit(solution)/shard_map/ppermute | solution.py:199
  221.0 13.9 collective-permute-done.32
  254.7 13.9 collective-permute-done.34
  288.4 13.9 collective-permute-done.36
  322.1 13.9 collective-permute-done.38
  355.8 13.9 collective-permute-done.40
  387.6 15.8 %collective-permute-done.42 = f32[128,1536]{1,0:T(8,128)S(1)} collective-permute-done((f32[128,1536]{1,0:T(8,128)S(1)}, f32[128,1536]{1,0:T(8,128)S(1)}, u32[]{:S(2)}, u32[]{:S(2)}) %collective-permute-start.42) | collective-permute-done | bytes 786464 | tf_op jit(solution)/shard_map/ppermute | solution.py:199
  407.3 26.1 %right_product.7 = f32[512,1536]{1,0:T(8,128)} custom-call(f32[4,2,768,768]{3,2,1,0:T(8,128)} %t_ref.11, f32[2048,1536]{1,0:T(8,128)} %constant_dynamic-update-slice_fusion.21.refs_0_.lr_ref, f32[2048,1536]{1,0:T(8,128)} %constant_dynamic-update-slice_fusion.44.refs_1_.lr_ref), custom_call_target="tpu_custom_call" | custom-call | flops 14495514624 | bytes 34603008 | tf_op jit(solution)/shard_map/right_product/pallas_call | solution.py:86
  433.5 26.2 %right_product.6 = f32[512,1536]{1,0:T(8,128)} custom-call(f32[4,2,768,768]{3,2,1,0:T(8,128)} %t_ref.11, f32[2048,1536]{1,0:T(8,128)} %constant_dynamic-update-slice_fusion.21.refs_0_.lr_ref, f32[2048,1536]{1,0:T(8,128)} %constant_dynamic-update-slice_fusion.44.refs_1_.lr_ref), custom_call_target="tpu_custom_call" | custom-call | flops 14495514624 | bytes 34603008 | tf_op jit(solution)/shard_map/right_product/pallas_call | solution.py:86
  459.7 26.2 %right_product.5 = f32[512,1536]{1,0:T(8,128)} custom-call(f32[4,2,768,768]{3,2,1,0:T(8,128)} %t_ref.11, f32[2048,1536]{1,0:T(8,128)} %constant_dynamic-update-slice_fusion.21.refs_0_.lr_ref, f32[2048,1536]{1,0:T(8,128)} %constant_dynamic-update-slice_fusion.44.refs_1_.lr_ref), custom_call_target="tpu_custom_call" | custom-call | flops 14495514624 | bytes 34603008 | tf_op jit(solution)/shard_map/right_product/pallas_call | solution.py:86
  486.4 26.2 %right_product.4 = f32[512,1536]{1,0:T(8,128)} custom-call(f32[4,2,768,768]{3,2,1,0:T(8,128)} %t_ref.11, f32[2048,1536]{1,0:T(8,128)} %constant_dynamic-update-slice_fusion.21.refs_0_.lr_ref, f32[2048,1536]{1,0:T(8,128)} %constant_dynamic-update-slice_fusion.44.refs_1_.lr_ref), custom_call_target="tpu_custom_call" | custom-call | flops 14495514624 | bytes 34603008 | tf_op jit(solution)/shard_map/right_product/pallas_call | solution.py:86
  512.7 39.0 %left_product.3 = f32[2048,1536]{1,0:T(8,128)} custom-call(f32[4,2,768,768]{3,2,1,0:T(8,128)} %t_ref.11, f32[2048,1536]{1,0:T(8,128)} %all-gather.3.cloned.1.call-done.l_ref.lc_ref), custom_call_target="tpu_custom_call" | custom-call | flops 28991029248 | bytes 47185920 | tf_op jit(solution)/shard_map/left_product/pallas_call | solution.py:46
  556.6 39.3 %left_product.2 = f32[2048,1536]{1,0:T(8,128)} custom-call(f32[4,2,768,768]{3,2,1,0:T(8,128)} %t_ref.11, f32[2048,1536]{1,0:T(8,128)} %all-gather.3.cloned.1.call-done.l_ref.lc_ref), custom_call_target="tpu_custom_call" | custom-call | flops 28991029248 | bytes 47185920 | tf_op jit(solution)/shard_map/left_product/pallas_call | solution.py:46
  603.9 14.1 collective-permute-done.16
  639.2 12.5 collective-permute-done.17
  657.5 11.1 collective-permute-done.48
  672.9 12.5 collective-permute-done.18
  691.2 11.1 collective-permute-done.49
  706.6 12.5 collective-permute-done.19
  790.5 70.2 %collective-permute-start.22 = (f32[128,1536]{1,0:T(8,128)}, f32[128,1536]{1,0:T(8,128)}, u32[]{:S(2)}, u32[]{:S(2)}) collective-permute-start(f32[128,1536]{1,0:T(8,128)} %get-tuple-element.31), channel_id=1, source_target_pairs={{0,2},{2,4},{4,6},{6,7},{7,5},{5,3},{3,1},{1,0},{8,10},{10,12},{12... | collective-permute-start | bytes 2359304 | tf_op jit(solution)/shard_map/ppermute | solution.py:214
  862.0 75.0 %collective-permute-done.59 = f32[128,1536]{1,0:T(8,128)} collective-permute-done((f32[128,1536]{1,0:T(8,128)}, f32[128,1536]{1,0:T(8,128)}, u32[]{:S(2)}, u32[]{:S(2)}) %collective-permute-start.59) | collective-permute-done | bytes 786464 | tf_op jit(solution)/shard_map/ppermute | solution.py:214
  939.1 14.8 collective-permute-done.29
  959.5 13.4 collective-permute-start.60
  972.9 20.7 %collective-permute-done.61 = f32[256,1536]{1,0:T(8,128)} collective-permute-done((f32[256,1536]{1,0:T(8,128)}, f32[256,1536]{1,0:T(8,128)}, u32[]{:S(2)}, u32[]{:S(2)}) %collective-permute-start.61) | collective-permute-done | bytes 1572896 | tf_op jit(solution)/shard_map/ppermute | solution.py:249
  1001.8 54.1 %collective-permute-start.62 = (f32[128,1536]{1,0:T(8,128)}, f32[128,1536]{1,0:T(8,128)}, u32[]{:S(2)}, u32[]{:S(2)}) collective-permute-start(f32[128,1536]{1,0:T(8,128)} %get-tuple-element.58), channel_id=1, source_target_pairs={{0,2},{2,4},{4,6},{6,7},{7,5},{5,3},{3,1},{1,0},{8,10},{10,12},{12... | collective-permute-start | bytes 2359304 | tf_op jit(solution)/shard_map/ppermute | solution.py:199
  1062.8 49.0 %collective-permute-start.76 = (f32[128,1536]{1,0:T(8,128)S(1)}, f32[128,1536]{1,0:T(8,128)S(1)}, u32[]{:S(2)}, u32[]{:S(2)}) collective-permute-start(f32[128,1536]{1,0:T(8,128)S(1)} %get-tuple-element.56), channel_id=1, source_target_pairs={{0,2},{2,4},{4,6},{6,7},{7,5},{5,3},{3,1},{1,0},{8,10},{10,12},{12... | collective-permute-start | bytes 2359304 | tf_op jit(solution)/shard_map/ppermute | solution.py:199
  1341.0 38.3 %shard_map.955.refs_0_ = f32[4,2,768,768]{3,2,1,0:T(8,128)} custom-call(f32[4,2,768,768]{3,2,1,0:T(8,128)} %k_ref.3, f32[2048,1536]{1,0:T(8,128)} %constant_dynamic-update-slice_fusion.21.refs_0_.lr_ref, f32[2048,1536]{1,0:T(8,128)} %all-gather.5.cloned.1.call-done.sc_ref), custom_call_target="tpu_custom_call" | custom-call | flops 28991029248 | bytes 69206016 | tf_op jit(solution)/shard_map/pallas_call | solution.py:146
  1379.3 38.3 %shard_map.956.k_ref = f32[4,2,768,768]{3,2,1,0:T(8,128)} custom-call(f32[4,2,768,768]{3,2,1,0:T(8,128)} %k_ref.3, f32[2048,1536]{1,0:T(8,128)} %constant_dynamic-update-slice_fusion.44.refs_1_.lr_ref, f32[2048,1536]{1,0:T(8,128)} %all-gather.5.cloned.1.call-done.sc_ref, f32[4,2,768,768]{3,2,1,0:T(8,128)} %shard_map.955.refs_0_), custom_call_target="tpu_custom_call", output_to_operand_aliasing={{}: (3, {})} | custom-call | flops 28991029248 | bytes 69206016 | tf_op jit(solution)/shard_map/pallas_call | solution.py:146
  1417.6 39.7 %shard_map.957.k_ref = f32[4,2,768,768]{3,2,1,0:T(8,128)} custom-call(f32[4]{0:T(128)} %dynamic_slice.439.left_ref, f32[2]{0:T(128)} %dynamic_slice.440.right_ref, f32[1,768]{1,0:T(1,128)} %broadcast_in_dim.8.vir_row_ref, f32[768,1]{1,0:T(8,128)} %broadcast_in_dim.10.vir_col_ref, ...), custom_call_target="tpu_custom_call", output_to_operand_aliasing={{}: (4, {})} | custom-call | flops 28991029248 | bytes 69206016 | tf_op jit(solution)/shard_map/pallas_call | solution.py:146
  1457.2 40.0 %shard_map.958 = f32[4,2,768,768]{3,2,1,0:T(8,128)} custom-call(f32[4]{0:T(128)} %dynamic_slice.439.left_ref, f32[2]{0:T(128)} %dynamic_slice.440.right_ref, f32[1,768]{1,0:T(1,128)} %broadcast_in_dim.8.vir_row_ref, f32[768,1]{1,0:T(8,128)} %broadcast_in_dim.10.vir_col_ref, f32[4,2,768,768]{3,2,1,0:T(8,128)} %shard_map.957.k_ref, ...), custom_call_target="tpu_custom_call", output_to_operand_aliasing={{}: (4, {})} | custom-call | flops 28991029248 | bytes 69206016 | tf_op jit(solution)/shard_map/pallas_call | solution.py:146
  (308 shorter events, 536.6 us)
Async XLA Ops:
  6.5 506.2 %all-gather.3.cloned.1.call-start = ((), (), s32[]{:S(2)}) async-start(), calls=%async_computation.4 | async-start | bytes 15728640 | tf_op jit(solution)/shard_map/all_gather | solution.py:260
  10.7 730.7 %reduce-scatter.11.cloned.1.call-start = ((), (), s32[]{:S(2)}) async-start(), calls=%async_computation.8 | async-start | bytes 3932160 | tf_op jit(solution)/shard_map/reduce_scatter | solution.py:270
  23.0 55.4 %collective-permute-start.1 = (f32[256,1536]{1,0:T(8,128)}, f32[256,1536]{1,0:T(8,128)S(1)}, u32[]{:S(2)}, u32[]{:S(2)}) collective-permute-start(f32[256,1536]{1,0:T(8,128)} %get-tuple-element.54), channel_id=1, source_target_pairs={{0,1},{1,0},{2,9},{3,8},{4,17},{5,16},{6,25},{7,24},{8,3},{9,2},{1... | collective-permute-start | bytes 4718600 | tf_op jit(solution)/shard_map/ppermute | solution.py:234
  26.1 52.3 %collective-permute-start = (f32[256,1536]{1,0:T(8,128)}, f32[256,1536]{1,0:T(8,128)S(1)}, u32[]{:S(2)}, u32[]{:S(2)}) collective-permute-start(f32[256,1536]{1,0:T(8,128)} %get-tuple-element.53), channel_id=1, source_target_pairs={{0,0},{1,1},{2,8},{3,9},{4,16},{5,17},{6,24},{7,25},{8,2},{9,3},{1... | collective-permute-start | bytes 4718600 | tf_op jit(solution)/shard_map/ppermute | solution.py:234
  81.9 115.5 %collective-permute-start.2 = (f32[128,1536]{1,0:T(8,128)}, f32[128,1536]{1,0:T(8,128)}, u32[]{:S(2)}, u32[]{:S(2)}) collective-permute-start(f32[128,1536]{1,0:T(8,128)} %get-tuple-element.62), channel_id=1, source_target_pairs={{0,2},{2,4},{4,6},{6,7},{7,5},{5,3},{3,1},{1,0},{8,10},{10,12},{12... | collective-permute-start | bytes 2359304 | tf_op jit(solution)/shard_map/ppermute | solution.py:199
  96.3 103.1 %collective-permute-start.3 = (f32[128,1536]{1,0:T(8,128)}, f32[128,1536]{1,0:T(8,128)}, u32[]{:S(2)}, u32[]{:S(2)}) collective-permute-start(f32[128,1536]{1,0:T(8,128)} %get-tuple-element.61), channel_id=1, source_target_pairs={{0,1},{2,0},{4,2},{6,4},{7,6},{5,7},{3,5},{1,3},{8,9},{10,8},{12,1... | collective-permute-start | bytes 2359304 | tf_op jit(solution)/shard_map/ppermute | solution.py:199
  104.1 95.3 %collective-permute-start.30 = (f32[128,1536]{1,0:T(8,128)S(1)}, f32[128,1536]{1,0:T(8,128)S(1)}, u32[]{:S(2)}, u32[]{:S(2)}) collective-permute-start(f32[128,1536]{1,0:T(8,128)S(1)} %get-tuple-element.60), channel_id=1, source_target_pairs={{0,2},{2,4},{4,6},{6,7},{7,5},{5,3},{3,1},{1,0},{8,10},{10,12},{12... | collective-permute-start | bytes 2359304 | tf_op jit(solution)/shard_map/ppermute | solution.py:199
  199.4 35.4 %collective-permute-start.32 = (f32[128,1536]{1,0:T(8,128)S(1)}, f32[128,1536]{1,0:T(8,128)S(1)}, u32[]{:S(2)}, u32[]{:S(2)}) collective-permute-start(f32[128,1536]{1,0:T(8,128)S(1)} %collective-permute-done.30), channel_id=1, source_target_pairs={{0,2},{2,4},{4,6},{6,7},{7,5},{5,3},{3,1},{1,0},{8,10},{10,12},{12... | collective-permute-start | bytes 2359304 | tf_op jit(solution)/shard_map/ppermute | solution.py:199
  218.0 33.7 %collective-permute-start.6 = (f32[128,1536]{1,0:T(8,128)S(1)}, f32[128,1536]{1,0:T(8,128)S(1)}, u32[]{:S(2)}, u32[]{:S(2)}) collective-permute-start(f32[128,1536]{1,0:T(8,128)S(1)} %collective-permute-done.4), channel_id=1, source_target_pairs={{0,2},{2,4},{4,6},{6,7},{7,5},{5,3},{3,1},{1,0},{8,10},{10,12},{12... | collective-permute-start | bytes 2359304 | tf_op jit(solution)/shard_map/ppermute | solution.py:199
  234.9 33.7 %collective-permute-start.34 = (f32[128,1536]{1,0:T(8,128)S(1)}, f32[128,1536]{1,0:T(8,128)S(1)}, u32[]{:S(2)}, u32[]{:S(2)}) collective-permute-start(f32[128,1536]{1,0:T(8,128)S(1)} %collective-permute-done.32), channel_id=1, source_target_pairs={{0,2},{2,4},{4,6},{6,7},{7,5},{5,3},{3,1},{1,0},{8,10},{10,12},{12... | collective-permute-start | bytes 2359304 | tf_op jit(solution)/shard_map/ppermute | solution.py:199
  338.9 35.2 %collective-permute-start.41 = (f32[128,1536]{1,0:T(8,128)S(1)}, f32[128,1536]{1,0:T(8,128)S(1)}, u32[]{:S(2)}, u32[]{:S(2)}) collective-permute-start(f32[128,1536]{1,0:T(8,128)S(1)} %collective-permute-done.39), channel_id=1, source_target_pairs={{0,1},{2,0},{4,2},{6,4},{7,6},{5,7},{3,5},{1,3},{8,9},{10,8},{12,1... | collective-permute-start | bytes 2359304 | tf_op jit(solution)/shard_map/ppermute | solution.py:199
  355.8 48.6 %collective-permute-start.15 = (f32[128,1536]{1,0:T(8,128)S(1)}, f32[128,1536]{1,0:T(8,128)S(1)}, u32[]{:S(2)}, u32[]{:S(2)}) collective-permute-start(f32[128,1536]{1,0:T(8,128)S(1)} %collective-permute-done.13), channel_id=1, source_target_pairs={{0,1},{2,0},{4,2},{6,4},{7,6},{5,7},{3,5},{1,3},{8,9},{10,8},{12,1... | collective-permute-start | bytes 2359304 | tf_op jit(solution)/shard_map/ppermute | solution.py:199
  433.4 307.9 %reduce-scatter.9.cloned.1.call-start = ((), (), s32[]{:S(2)}) async-start(), calls=%async_computation.7 | async-start | bytes 3932160 | tf_op jit(solution)/shard_map/reduce_scatter | solution.py:270
  459.7 281.7 %reduce-scatter.7.cloned.1.call-start = ((), (), s32[]{:S(2)}) async-start(), calls=%async_computation.6 | async-start | bytes 3932160 | tf_op jit(solution)/shard_map/reduce_scatter | solution.py:270
  486.0 255.4 %reduce-scatter.5.cloned.1.call-start = ((), (), s32[]{:S(2)}) async-start(), calls=%async_computation.5 | async-start | bytes 3932160 | tf_op jit(solution)/shard_map/reduce_scatter | solution.py:270
  512.7 828.3 %all-gather.5.cloned.1.call-start = ((), (), s32[]{:S(2)}) async-start(), calls=%async_computation.9 | async-start | bytes 15728640 | tf_op jit(solution)/shard_map/all_gather | solution.py:273
  554.4 45.2 %collective-permute-start.46 = (f32[128,1536]{1,0:T(8,128)}, f32[128,1536]{1,0:T(8,128)S(1)}, u32[]{:S(2)}, u32[]{:S(2)}) collective-permute-start(f32[128,1536]{1,0:T(8,128)} %get-tuple-element.27), channel_id=1, source_target_pairs={{0,2},{2,4},{4,6},{6,7},{7,5},{5,3},{3,1},{1,0},{8,10},{10,12},{12... | collective-permute-start | bytes 2359304 | tf_op jit(solution)/shard_map/ppermute | solution.py:214
  556.6 43.1 %collective-permute-start.53 = (f32[128,1536]{1,0:T(8,128)}, f32[128,1536]{1,0:T(8,128)}, u32[]{:S(2)}, u32[]{:S(2)}) collective-permute-start(f32[128,1536]{1,0:T(8,128)} %get-tuple-element.28), channel_id=1, source_target_pairs={{0,1},{2,0},{4,2},{6,4},{7,6},{5,7},{3,5},{1,3},{8,9},{10,8},{12,1... | collective-permute-start | bytes 2359304 | tf_op jit(solution)/shard_map/ppermute | solution.py:214
  774.6 86.1 %collective-permute-start.52 = (f32[128,1536]{1,0:T(8,128)S(1)}, f32[128,1536]{1,0:T(8,128)}, u32[]{:S(2)}, u32[]{:S(2)}) collective-permute-start(f32[128,1536]{1,0:T(8,128)S(1)} %get-tuple-element.15), channel_id=1, source_target_pairs={{0,2},{2,4},{4,6},{6,7},{7,5},{5,3},{3,1},{1,0},{8,10},{10,12},{12... | collective-permute-start | bytes 2359304 | tf_op jit(solution)/shard_map/ppermute | solution.py:214
  778.4 177.6 %collective-permute-start.45 = (f32[256,1536]{1,0:T(8,128)}, f32[256,1536]{1,0:T(8,128)S(1)}, u32[]{:S(2)}, u32[]{:S(2)}) collective-permute-start(f32[256,1536]{1,0:T(8,128)} %get-tuple-element.52), channel_id=1, source_target_pairs={{0,1},{1,0},{2,9},{3,8},{4,17},{5,16},{6,25},{7,24},{8,3},{9,2},{1... | collective-permute-start | bytes 4718600 | tf_op jit(solution)/shard_map/ppermute | solution.py:234
  778.5 177.5 %collective-permute-start.44 = (f32[256,1536]{1,0:T(8,128)}, f32[256,1536]{1,0:T(8,128)S(1)}, u32[]{:S(2)}, u32[]{:S(2)}) collective-permute-start(f32[256,1536]{1,0:T(8,128)} %get-tuple-element.51), channel_id=1, source_target_pairs={{0,0},{1,1},{2,8},{3,9},{4,16},{5,17},{6,24},{7,25},{8,2},{9,3},{1... | collective-permute-start | bytes 4718600 | tf_op jit(solution)/shard_map/ppermute | solution.py:234
  786.5 150.5 %collective-permute-start.59 = (f32[128,1536]{1,0:T(8,128)}, f32[128,1536]{1,0:T(8,128)}, u32[]{:S(2)}, u32[]{:S(2)}) collective-permute-start(f32[128,1536]{1,0:T(8,128)} %get-tuple-element.16), channel_id=1, source_target_pairs={{0,1},{2,0},{4,2},{6,4},{7,6},{5,7},{3,5},{1,3},{8,9},{10,8},{12,1... | collective-permute-start | bytes 2359304 | tf_op jit(solution)/shard_map/ppermute | solution.py:214
  790.5 148.6 %collective-permute-start.22 = (f32[128,1536]{1,0:T(8,128)}, f32[128,1536]{1,0:T(8,128)}, u32[]{:S(2)}, u32[]{:S(2)}) collective-permute-start(f32[128,1536]{1,0:T(8,128)} %get-tuple-element.31), channel_id=1, source_target_pairs={{0,2},{2,4},{4,6},{6,7},{7,5},{5,3},{3,1},{1,0},{8,10},{10,12},{12... | collective-permute-start | bytes 2359304 | tf_op jit(solution)/shard_map/ppermute | solution.py:214
  860.7 93.2 %collective-permute-start.29 = (f32[128,1536]{1,0:T(8,128)}, f32[128,1536]{1,0:T(8,128)}, u32[]{:S(2)}, u32[]{:S(2)}) collective-permute-start(f32[128,1536]{1,0:T(8,128)} %get-tuple-element.32), channel_id=1, source_target_pairs={{0,1},{2,0},{4,2},{6,4},{7,6},{5,7},{3,5},{1,3},{8,9},{10,8},{12,1... | collective-permute-start | bytes 2359304 | tf_op jit(solution)/shard_map/ppermute | solution.py:214
  1001.8 112.8 %collective-permute-start.62 = (f32[128,1536]{1,0:T(8,128)}, f32[128,1536]{1,0:T(8,128)}, u32[]{:S(2)}, u32[]{:S(2)}) collective-permute-start(f32[128,1536]{1,0:T(8,128)} %get-tuple-element.58), channel_id=1, source_target_pairs={{0,2},{2,4},{4,6},{6,7},{7,5},{5,3},{3,1},{1,0},{8,10},{10,12},{12... | collective-permute-start | bytes 2359304 | tf_op jit(solution)/shard_map/ppermute | solution.py:199
  1055.9 66.8 %collective-permute-start.63 = (f32[128,1536]{1,0:T(8,128)}, f32[128,1536]{1,0:T(8,128)}, u32[]{:S(2)}, u32[]{:S(2)}) collective-permute-start(f32[128,1536]{1,0:T(8,128)} %get-tuple-element.57), channel_id=1, source_target_pairs={{0,1},{2,0},{4,2},{6,4},{7,6},{5,7},{3,5},{1,3},{8,9},{10,8},{12,1... | collective-permute-start | bytes 2359304 | tf_op jit(solution)/shard_map/ppermute | solution.py:199
  1062.8 66.3 %collective-permute-start.76 = (f32[128,1536]{1,0:T(8,128)S(1)}, f32[128,1536]{1,0:T(8,128)S(1)}, u32[]{:S(2)}, u32[]{:S(2)}) collective-permute-start(f32[128,1536]{1,0:T(8,128)S(1)} %get-tuple-element.56), channel_id=1, source_target_pairs={{0,2},{2,4},{4,6},{6,7},{7,5},{5,3},{3,1},{1,0},{8,10},{10,12},{12... | collective-permute-start | bytes 2359304 | tf_op jit(solution)/shard_map/ppermute | solution.py:199
  1171.9 33.7 %collective-permute-start.81 = (f32[128,1536]{1,0:T(8,128)S(1)}, f32[128,1536]{1,0:T(8,128)S(1)}, u32[]{:S(2)}, u32[]{:S(2)}) collective-permute-start(f32[128,1536]{1,0:T(8,128)S(1)} %collective-permute-done.79), channel_id=1, source_target_pairs={{0,1},{2,0},{4,2},{6,4},{7,6},{5,7},{3,5},{1,3},{8,9},{10,8},{12,1... | collective-permute-start | bytes 2359304 | tf_op jit(solution)/shard_map/ppermute | solution.py:199
  1188.8 33.7 %collective-permute-start.69 = (f32[128,1536]{1,0:T(8,128)S(1)}, f32[128,1536]{1,0:T(8,128)S(1)}, u32[]{:S(2)}, u32[]{:S(2)}) collective-permute-start(f32[128,1536]{1,0:T(8,128)S(1)} %collective-permute-done.67), channel_id=1, source_target_pairs={{0,1},{2,0},{4,2},{6,4},{7,6},{5,7},{3,5},{1,3},{8,9},{10,8},{12,1... | collective-permute-start | bytes 2359304 | tf_op jit(solution)/shard_map/ppermute | solution.py:199
  1205.7 33.7 %collective-permute-start.83 = (f32[128,1536]{1,0:T(8,128)S(1)}, f32[128,1536]{1,0:T(8,128)S(1)}, u32[]{:S(2)}, u32[]{:S(2)}) collective-permute-start(f32[128,1536]{1,0:T(8,128)S(1)} %collective-permute-done.81), channel_id=1, source_target_pairs={{0,1},{2,0},{4,2},{6,4},{7,6},{5,7},{3,5},{1,3},{8,9},{10,8},{12,1... | collective-permute-start | bytes 2359304 | tf_op jit(solution)/shard_map/ppermute | solution.py:199
  1222.5 33.7 %collective-permute-start.71 = (f32[128,1536]{1,0:T(8,128)S(1)}, f32[128,1536]{1,0:T(8,128)S(1)}, u32[]{:S(2)}, u32[]{:S(2)}) collective-permute-start(f32[128,1536]{1,0:T(8,128)S(1)} %collective-permute-done.69), channel_id=1, source_target_pairs={{0,1},{2,0},{4,2},{6,4},{7,6},{5,7},{3,5},{1,3},{8,9},{10,8},{12,1... | collective-permute-start | bytes 2359304 | tf_op jit(solution)/shard_map/ppermute | solution.py:199
  1273.1 33.7 %collective-permute-start.87 = (f32[128,1536]{1,0:T(8,128)S(1)}, f32[128,1536]{1,0:T(8,128)S(1)}, u32[]{:S(2)}, u32[]{:S(2)}) collective-permute-start(f32[128,1536]{1,0:T(8,128)S(1)} %collective-permute-done.85), channel_id=1, source_target_pairs={{0,1},{2,0},{4,2},{6,4},{7,6},{5,7},{3,5},{1,3},{8,9},{10,8},{12,1... | collective-permute-start | bytes 2359304 | tf_op jit(solution)/shard_map/ppermute | solution.py:199
  (80 other events, 2698.5 us)
Sparse Core Ops, SparseCore 0:
  10.8 142.1 all-gather.2
  433.6 37.0 reduce-scatter.10
  473.2 37.9 reduce-scatter.8
  513.5 37.8 reduce-scatter.6
  553.8 37.9 reduce-scatter.4
  998.2 182.7 all-gather.4
where the time goes:
time: 1520 us; the launch traced here: 1500 us
  waiting for transfers between devices  554 us (36%)
  starting transfers between devices  438 us (29%)
  Pallas kernels  339 us (22%)
  local copies, waits for them, and re-layouts  103 us (7%)
  other arithmetic  35.6 us (2%)
  between operations  34.7 us (2%)
    ppermute x56, starting transfers between devices, ring_gather(): held[k] = lax.ppermute(held[k], 'col', perm)  319 us
    ppermute x56, waiting for transfers between devices, ring_gather(): held[k] = lax.ppermute(held[k], 'col', perm)  249 us
    ppermute x28, waiting for transfers between devices, ring_scatter(): held = lax.ppermute(held, 'col', perm)  233 us
    pallas_call x4, Pallas kernels, tile_call(): pl.pallas_call(kernel, grid=(own, oj, aux // block), in_specs=specs, out_...  156 us
    pallas_call x4, Pallas kernels, right_product(): pl.pallas_call(functools.partial(right_kernel, oi, vir, parts), grid=(oj,...  105 us
    ppermute x28, starting transfers between devices, ring_scatter(): held = lax.ppermute(held, 'col', perm)  97.2 us
    pallas_call x2, Pallas kernels, left_product(): pl.pallas_call(functools.partial(left_kernel, min(256, block), oj, vir),...  78.4 us
    dynamic_update_slice x56, local copies, waits for them, and re-layouts, ring_gather(): lax.dynamic_update_slice(full, held[k], (owner(step) * 2 * half + k * hal...  58 us
  transfers between devices with their start and end apart: 96, of which 64 were waited for; matrix products, arithmetic and copies ran while one was open for 8% of the time, Pallas kernels for 12%

commit v1 on v0

--- a/solution.py
+++ b/solution.py
@@ -268,9 +268,11 @@
     for h in range(pieces):
         right.append(right_product(amplitudes, fac_row, rows, h, pieces))
     right = [lax.psum_scatter(piece, "row", scatter_dimension=0, tiled=True) for piece in right]
-    right = to_row(jnp.concatenate(right, axis=0), rows, cols)
-    summed = [2.0 * left[g] - right[:, g * wide:(g + 1) * wide] for g in range(parts)]
-    sum_col = lax.all_gather(to_col(jnp.concatenate(summed, axis=1), rows, cols), "row", axis=0, tiled=True)
+    right = jnp.concatenate(right, axis=0)
+    across = to_row(right, rows, cols)
+    summed = [2.0 * left[g] - across[:, g * wide:(g + 1) * wide] for g in range(parts)]
+    back = 2.0 * to_col(jnp.concatenate(left, axis=1), rows, cols) - right
+    sum_col = lax.all_gather(back, "row", axis=0, tiled=True)
     sum_row = [ring_gather(part, cols) for part in summed]
     occ_left = lax.dynamic_slice_in_dim(occ_energy, lax.axis_index("row") * oi, oi)
     occ_right = lax.dynamic_slice_in_dim(occ_energy, lax.axis_index("col") * oj, oj)

time: 1520 us -> 1520 us (level)
  waiting for transfers between devices: 554 us -> 390 us
  starting transfers between devices: 438 us -> 574 us
  other arithmetic: 35.6 us -> 54.6 us
    ppermute x56, waiting for transfers between devices: 249 us -> 163 us  [ring_gather(): held[k] = lax.ppermute(held[k], 'col', perm)]
    ppermute x56, starting transfers between devices: 319 us -> 401 us  [ring_gather(): held[k] = lax.ppermute(held[k], 'col', perm)]
    ppermute x28, waiting for transfers between devices: 233 us -> 158 us  [ring_scatter(): held = lax.ppermute(held, 'col', perm)]
    ppermute x28, starting transfers between devices: 97.2 us -> 129 us  [ring_scatter(): held = lax.ppermute(held, 'col', perm)]
    ppermute x4, waiting for transfers between devices: 50.1 us -> 18.6 us  [to_row(): lax.ppermute(pick(parts, lax.rem(col + k, ratio)), ('row', 'col'), perm)]
    ppermute x2, waiting for transfers between devices: 20.7 us -> 50.2 us  [to_col(): lax.ppermute(pick(parts, lax.rem(col + ratio - k, ratio)), ('row', 'col')...]
    add x14, other arithmetic: 22.6 us -> 38.4 us  [ring_scatter(): held = held + mine(step + 1)]
  transfers between devices with their start and end apart: 96 -> 96, of which waited for: 64 -> 49; matrix products, arithmetic and copies ran while one was open for 8% -> 9% of each run, Pallas kernels for 12% -> 12%
where the time goes in v1:
time: 1520 us; the launch traced here: 1500 us
  starting transfers between devices  574 us (38%)
  waiting for transfers between devices  390 us (26%)
  Pallas kernels  339 us (22%)
  local copies, waits for them, and re-layouts  109 us (7%)
  other arithmetic  54.6 us (4%)
  between operations  33.2 us (2%)
    ppermute x56, starting transfers between devices, ring_gather(): held[k] = lax.ppermute(held[k], 'col', perm)  401 us
    ppermute x56, waiting for transfers between devices, ring_gather(): held[k] = lax.ppermute(held[k], 'col', perm)  163 us
    ppermute x28, waiting for transfers between devices, ring_scatter(): held = lax.ppermute(held, 'col', perm)  158 us
    pallas_call x4, Pallas kernels, tile_call(): pl.pallas_call(kernel, grid=(own, oj, aux // block), in_specs=specs, out_...  157 us
    ppermute x28, starting transfers between devices, ring_scatter(): held = lax.ppermute(held, 'col', perm)  129 us
    pallas_call x4, Pallas kernels, right_product(): pl.pallas_call(functools.partial(right_kernel, oi, vir, parts), grid=(oj,...  105 us
    pallas_call x2, Pallas kernels, left_product(): pl.pallas_call(functools.partial(left_kernel, min(256, block), oj, vir),...  77.6 us
    dynamic_update_slice x56, local copies, waits for them, and re-layouts, ring_gather(): lax.dynamic_update_slice(full, held[k], (owner(step) * 2 * half + k * hal...  55.7 us
  transfers between devices with their start and end apart: 96, of which 49 were waited for; matrix products, arithmetic and copies ran while one was open for 9% of the time, Pallas kernels for 12%

profile of v1, /device:TPU:0, one launch (start us, length us, event | category | flops | bytes accessed | tf_op | source)
XLA Modules:
  0.0 1499.4 jit_solution(10195742819808438909)
XLA Ops:
  28.1 18.6 %collective-permute-done.1 = f32[256,1536]{1,0:T(8,128)S(1)} collective-permute-done((f32[256,1536]{1,0:T(8,128)}, f32[256,1536]{1,0:T(8,128)S(1)}, u32[]{:S(2)}, u32[]{:S(2)}) %collective-permute-start.1) | collective-permute-done | bytes 1572896 | tf_op jit(solution)/shard_map/ppermute | solution.py:234
  50.2 47.1 %collective-permute-start.46 = (f32[128,1536]{1,0:T(8,128)}, f32[128,1536]{1,0:T(8,128)}, u32[]{:S(2)}, u32[]{:S(2)}) collective-permute-start(f32[128,1536]{1,0:T(8,128)} %get-tuple-element.60), channel_id=1, source_target_pairs={{0,2},{2,4},{4,6},{6,7},{7,5},{5,3},{3,1},{1,0},{8,10},{10,12},{12... | collective-permute-start | bytes 2359304 | tf_op jit(solution)/shard_map/ppermute | solution.py:199
  105.0 72.7 %collective-permute-start.2 = (f32[128,1536]{1,0:T(8,128)S(1)}, f32[128,1536]{1,0:T(8,128)S(1)}, u32[]{:S(2)}, u32[]{:S(2)}) collective-permute-start(f32[128,1536]{1,0:T(8,128)S(1)} %get-tuple-element.62), channel_id=1, source_target_pairs={{0,2},{2,4},{4,6},{6,7},{7,5},{5,3},{3,1},{1,0},{8,10},{10,12},{12... | collective-permute-start | bytes 2359304 | tf_op jit(solution)/shard_map/ppermute | solution.py:199
  221.0 12.7 collective-permute-done.4
  254.7 12.7 collective-permute-done.6
  288.4 12.7 collective-permute-done.8
  322.1 12.7 collective-permute-done.10
  355.8 12.7 collective-permute-done.12
  386.3 15.9 %collective-permute-done.14 = f32[128,1536]{1,0:T(8,128)S(1)} collective-permute-done((f32[128,1536]{1,0:T(8,128)S(1)}, f32[128,1536]{1,0:T(8,128)S(1)}, u32[]{:S(2)}, u32[]{:S(2)}) %collective-permute-start.14) | collective-permute-done | bytes 786464 | tf_op jit(solution)/shard_map/ppermute | solution.py:199
  407.4 26.1 %right_product.4 = f32[512,1536]{1,0:T(8,128)} custom-call(f32[4,2,768,768]{3,2,1,0:T(8,128)} %t_ref.11, f32[2048,1536]{1,0:T(8,128)} %constant_dynamic-update-slice_fusion.7.refs_0_.lr_ref, f32[2048,1536]{1,0:T(8,128)} %constant_dynamic-update-slice_fusion.44.refs_1_.lr_ref), custom_call_target="tpu_custom_call" | custom-call | flops 14495514624 | bytes 34603008 | tf_op jit(solution)/shard_map/right_product/pallas_call | solution.py:86
  433.6 26.1 %right_product.5 = f32[512,1536]{1,0:T(8,128)} custom-call(f32[4,2,768,768]{3,2,1,0:T(8,128)} %t_ref.11, f32[2048,1536]{1,0:T(8,128)} %constant_dynamic-update-slice_fusion.7.refs_0_.lr_ref, f32[2048,1536]{1,0:T(8,128)} %constant_dynamic-update-slice_fusion.44.refs_1_.lr_ref), custom_call_target="tpu_custom_call" | custom-call | flops 14495514624 | bytes 34603008 | tf_op jit(solution)/shard_map/right_product/pallas_call | solution.py:86
  459.8 26.2 %right_product.6 = f32[512,1536]{1,0:T(8,128)} custom-call(f32[4,2,768,768]{3,2,1,0:T(8,128)} %t_ref.11, f32[2048,1536]{1,0:T(8,128)} %constant_dynamic-update-slice_fusion.7.refs_0_.lr_ref, f32[2048,1536]{1,0:T(8,128)} %constant_dynamic-update-slice_fusion.44.refs_1_.lr_ref), custom_call_target="tpu_custom_call" | custom-call | flops 14495514624 | bytes 34603008 | tf_op jit(solution)/shard_map/right_product/pallas_call | solution.py:86
  486.5 26.3 %right_product.7 = f32[512,1536]{1,0:T(8,128)} custom-call(f32[4,2,768,768]{3,2,1,0:T(8,128)} %t_ref.11, f32[2048,1536]{1,0:T(8,128)} %constant_dynamic-update-slice_fusion.7.refs_0_.lr_ref, f32[2048,1536]{1,0:T(8,128)} %constant_dynamic-update-slice_fusion.44.refs_1_.lr_ref), custom_call_target="tpu_custom_call" | custom-call | flops 14495514624 | bytes 34603008 | tf_op jit(solution)/shard_map/right_product/pallas_call | solution.py:86
  512.9 38.8 %left_product.3 = f32[2048,1536]{1,0:T(8,128)} custom-call(f32[4,2,768,768]{3,2,1,0:T(8,128)} %t_ref.11, f32[2048,1536]{1,0:T(8,128)} %all-gather.3.cloned.1.call-done.l_ref.lc_ref), custom_call_target="tpu_custom_call" | custom-call | flops 28991029248 | bytes 47185920 | tf_op jit(solution)/shard_map/left_product/pallas_call | solution.py:46
  556.6 38.8 %left_product.2 = f32[2048,1536]{1,0:T(8,128)} custom-call(f32[4,2,768,768]{3,2,1,0:T(8,128)} %t_ref.11, f32[2048,1536]{1,0:T(8,128)} %all-gather.3.cloned.1.call-done.l_ref.lc_ref), custom_call_target="tpu_custom_call" | custom-call | flops 28991029248 | bytes 47185920 | tf_op jit(solution)/shard_map/left_product/pallas_call | solution.py:46
  604.1 13.2 collective-permute-done.16
  761.0 13.3 collective-permute-start.60
  779.1 64.0 %collective-permute-start.36 = (f32[128,1536]{1,0:T(8,128)}, f32[128,1536]{1,0:T(8,128)}, u32[]{:S(2)}, u32[]{:S(2)}) collective-permute-start(f32[128,1536]{1,0:T(8,128)} %get-tuple-element.15), channel_id=1, source_target_pairs={{0,2},{2,4},{4,6},{6,7},{7,5},{5,3},{3,1},{1,0},{8,10},{10,12},{12... | collective-permute-start | bytes 2359304 | tf_op jit(solution)/shard_map/ppermute | solution.py:214
  844.4 42.4 %collective-permute-done.28 = f32[128,1536]{1,0:T(8,128)} collective-permute-done((f32[128,1536]{1,0:T(8,128)}, f32[128,1536]{1,0:T(8,128)}, u32[]{:S(2)}, u32[]{:S(2)}) %collective-permute-start.28) | collective-permute-done | bytes 786464 | tf_op jit(solution)/shard_map/ppermute | solution.py:214
  888.8 38.0 %collective-permute-start.22 = (f32[128,1536]{1,0:T(8,128)S(1)}, f32[128,1536]{1,0:T(8,128)S(1)}, u32[]{:S(2)}, u32[]{:S(2)}) collective-permute-start(f32[128,1536]{1,0:T(8,128)S(1)} %get-tuple-element.31), channel_id=1, source_target_pairs={{0,2},{2,4},{4,6},{6,7},{7,5},{5,3},{3,1},{1,0},{8,10},{10,12},{12... | collective-permute-start | bytes 2359304 | tf_op jit(solution)/shard_map/ppermute | solution.py:214
  958.6 13.3 collective-permute-start.44
  971.9 11.9 collective-permute-start.45
  983.8 50.2 %collective-permute-done.45 = f32[256,1536]{1,0:T(8,128)} collective-permute-done((f32[256,1536]{1,0:T(8,128)}, f32[256,1536]{1,0:T(8,128)}, u32[]{:S(2)}, u32[]{:S(2)}) %collective-permute-start.45) | collective-permute-done | bytes 1572896 | tf_op jit(solution)/shard_map/ppermute | solution.py:249
  1048.2 60.8 %collective-permute-start.62 = (f32[128,1536]{1,0:T(8,128)}, f32[128,1536]{1,0:T(8,128)S(1)}, u32[]{:S(2)}, u32[]{:S(2)}) collective-permute-start(f32[128,1536]{1,0:T(8,128)} %get-tuple-element.57), channel_id=1, source_target_pairs={{0,2},{2,4},{4,6},{6,7},{7,5},{5,3},{3,1},{1,0},{8,10},{10,12},{12... | collective-permute-start | bytes 2359304 | tf_op jit(solution)/shard_map/ppermute | solution.py:199
  1137.8 10.9 collective-permute-start.80
  1188.3 10.9 collective-permute-start.68
  1238.9 10.9 collective-permute-start.86
  1272.6 11.2 collective-permute-start.88
  1335.5 38.3 %shard_map.955.refs_0_ = f32[4,2,768,768]{3,2,1,0:T(8,128)} custom-call(f32[4,2,768,768]{3,2,1,0:T(8,128)} %k_ref.3, f32[2048,1536]{1,0:T(8,128)} %constant_dynamic-update-slice_fusion.7.refs_0_.lr_ref, f32[2048,1536]{1,0:T(8,128)} %all-gather.5.cloned.1.call-done.sc_ref), custom_call_target="tpu_custom_call" | custom-call | flops 28991029248 | bytes 69206016 | tf_op jit(solution)/shard_map/pallas_call | solution.py:146
  1373.8 38.3 %shard_map.956.k_ref = f32[4,2,768,768]{3,2,1,0:T(8,128)} custom-call(f32[4,2,768,768]{3,2,1,0:T(8,128)} %k_ref.3, f32[2048,1536]{1,0:T(8,128)} %constant_dynamic-update-slice_fusion.44.refs_1_.lr_ref, f32[2048,1536]{1,0:T(8,128)} %all-gather.5.cloned.1.call-done.sc_ref, f32[4,2,768,768]{3,2,1,0:T(8,128)} %shard_map.955.refs_0_), custom_call_target="tpu_custom_call", output_to_operand_aliasing={{}: (3, {})} | custom-call | flops 28991029248 | bytes 69206016 | tf_op jit(solution)/shard_map/pallas_call | solution.py:146
  1412.1 39.7 %shard_map.957.k_ref = f32[4,2,768,768]{3,2,1,0:T(8,128)} custom-call(f32[4]{0:T(128)} %dynamic_slice.439.left_ref, f32[2]{0:T(128)} %dynamic_slice.440.right_ref, f32[1,768]{1,0:T(1,128)} %broadcast_in_dim.8.vir_row_ref, f32[768,1]{1,0:T(8,128)} %broadcast_in_dim.10.vir_col_ref, ...), custom_call_target="tpu_custom_call", output_to_operand_aliasing={{}: (4, {})} | custom-call | flops 28991029248 | bytes 69206016 | tf_op jit(solution)/shard_map/pallas_call | solution.py:146
  1451.8 40.3 %shard_map.958 = f32[4,2,768,768]{3,2,1,0:T(8,128)} custom-call(f32[4]{0:T(128)} %dynamic_slice.439.left_ref, f32[2]{0:T(128)} %dynamic_slice.440.right_ref, f32[1,768]{1,0:T(1,128)} %broadcast_in_dim.8.vir_row_ref, f32[768,1]{1,0:T(8,128)} %broadcast_in_dim.10.vir_col_ref, f32[4,2,768,768]{3,2,1,0:T(8,128)} %shard_map.957.k_ref, ...), custom_call_target="tpu_custom_call", output_to_operand_aliasing={{}: (4, {})} | custom-call | flops 28991029248 | bytes 69206016 | tf_op jit(solution)/shard_map/pallas_call | solution.py:146
  (290 shorter events, 558.6 us)
Async XLA Ops:
  6.5 506.4 %all-gather.3.cloned.1.call-start = ((), (), s32[]{:S(2)}) async-start(), calls=%async_computation.4 | async-start | bytes 15728640 | tf_op jit(solution)/shard_map/all_gather | solution.py:260
  10.6 613.5 %reduce-scatter.5.cloned.1.call-start = ((), (), s32[]{:S(2)}) async-start(), calls=%async_computation.5 | async-start | bytes 3932160 | tf_op jit(solution)/shard_map/reduce_scatter | solution.py:270
  50.2 146.7 %collective-permute-start.46 = (f32[128,1536]{1,0:T(8,128)}, f32[128,1536]{1,0:T(8,128)}, u32[]{:S(2)}, u32[]{:S(2)}) collective-permute-start(f32[128,1536]{1,0:T(8,128)} %get-tuple-element.60), channel_id=1, source_target_pairs={{0,2},{2,4},{4,6},{6,7},{7,5},{5,3},{3,1},{1,0},{8,10},{10,12},{12... | collective-permute-start | bytes 2359304 | tf_op jit(solution)/shard_map/ppermute | solution.py:199
  97.3 101.6 %collective-permute-start.47 = (f32[128,1536]{1,0:T(8,128)}, f32[128,1536]{1,0:T(8,128)}, u32[]{:S(2)}, u32[]{:S(2)}) collective-permute-start(f32[128,1536]{1,0:T(8,128)} %get-tuple-element.59), channel_id=1, source_target_pairs={{0,1},{2,0},{4,2},{6,4},{7,6},{5,7},{3,5},{1,3},{8,9},{10,8},{12,1... | collective-permute-start | bytes 2359304 | tf_op jit(solution)/shard_map/ppermute | solution.py:199
  105.0 93.9 %collective-permute-start.2 = (f32[128,1536]{1,0:T(8,128)S(1)}, f32[128,1536]{1,0:T(8,128)S(1)}, u32[]{:S(2)}, u32[]{:S(2)}) collective-permute-start(f32[128,1536]{1,0:T(8,128)S(1)} %get-tuple-element.62), channel_id=1, source_target_pairs={{0,2},{2,4},{4,6},{6,7},{7,5},{5,3},{3,1},{1,0},{8,10},{10,12},{12... | collective-permute-start | bytes 2359304 | tf_op jit(solution)/shard_map/ppermute | solution.py:199
  198.9 34.7 %collective-permute-start.4 = (f32[128,1536]{1,0:T(8,128)S(1)}, f32[128,1536]{1,0:T(8,128)S(1)}, u32[]{:S(2)}, u32[]{:S(2)}) collective-permute-start(f32[128,1536]{1,0:T(8,128)S(1)} %collective-permute-done.2), channel_id=1, source_target_pairs={{0,2},{2,4},{4,6},{6,7},{7,5},{5,3},{3,1},{1,0},{8,10},{10,12},{12... | collective-permute-start | bytes 2359304 | tf_op jit(solution)/shard_map/ppermute | solution.py:199
  339.0 35.1 %collective-permute-start.13 = (f32[128,1536]{1,0:T(8,128)S(1)}, f32[128,1536]{1,0:T(8,128)S(1)}, u32[]{:S(2)}, u32[]{:S(2)}) collective-permute-start(f32[128,1536]{1,0:T(8,128)S(1)} %collective-permute-done.11), channel_id=1, source_target_pairs={{0,1},{2,0},{4,2},{6,4},{7,6},{5,7},{3,5},{1,3},{8,9},{10,8},{12,1... | collective-permute-start | bytes 2359304 | tf_op jit(solution)/shard_map/ppermute | solution.py:199
  355.8 47.3 %collective-permute-start.59 = (f32[128,1536]{1,0:T(8,128)S(1)}, f32[128,1536]{1,0:T(8,128)S(1)}, u32[]{:S(2)}, u32[]{:S(2)}) collective-permute-start(f32[128,1536]{1,0:T(8,128)S(1)} %collective-permute-done.57), channel_id=1, source_target_pairs={{0,1},{2,0},{4,2},{6,4},{7,6},{5,7},{3,5},{1,3},{8,9},{10,8},{12,1... | collective-permute-start | bytes 2359304 | tf_op jit(solution)/shard_map/ppermute | solution.py:199
  433.5 224.8 %reduce-scatter.7.cloned.1.call-start = ((), (), s32[]{:S(2)}) async-start(), calls=%async_computation.6 | async-start | bytes 3932160 | tf_op jit(solution)/shard_map/reduce_scatter | solution.py:270
  459.7 232.3 %reduce-scatter.9.cloned.1.call-start = ((), (), s32[]{:S(2)}) async-start(), calls=%async_computation.7 | async-start | bytes 3932160 | tf_op jit(solution)/shard_map/reduce_scatter | solution.py:270
  486.0 239.9 %reduce-scatter.11.cloned.1.call-start = ((), (), s32[]{:S(2)}) async-start(), calls=%async_computation.8 | async-start | bytes 3932160 | tf_op jit(solution)/shard_map/reduce_scatter | solution.py:270
  512.8 822.6 %all-gather.5.cloned.1.call-start = ((), (), s32[]{:S(2)}) async-start(), calls=%async_computation.9 | async-start | bytes 15728640 | tf_op jit(solution)/shard_map/all_gather | solution.py:275
  554.4 44.6 %collective-permute-start.30 = (f32[128,1536]{1,0:T(8,128)}, f32[128,1536]{1,0:T(8,128)S(1)}, u32[]{:S(2)}, u32[]{:S(2)}) collective-permute-start(f32[128,1536]{1,0:T(8,128)} %get-tuple-element.27), channel_id=1, source_target_pairs={{0,2},{2,4},{4,6},{6,7},{7,5},{5,3},{3,1},{1,0},{8,10},{10,12},{12... | collective-permute-start | bytes 2359304 | tf_op jit(solution)/shard_map/ppermute | solution.py:214
  556.6 42.4 %collective-permute-start.37 = (f32[128,1536]{1,0:T(8,128)}, f32[128,1536]{1,0:T(8,128)}, u32[]{:S(2)}, u32[]{:S(2)}) collective-permute-start(f32[128,1536]{1,0:T(8,128)} %get-tuple-element.28), channel_id=1, source_target_pairs={{0,1},{2,0},{4,2},{6,4},{7,6},{5,7},{3,5},{1,3},{8,9},{10,8},{12,1... | collective-permute-start | bytes 2359304 | tf_op jit(solution)/shard_map/ppermute | solution.py:214
  739.4 34.9 %collective-permute-start.35 = (f32[128,1536]{1,0:T(8,128)S(1)}, f32[128,1536]{1,0:T(8,128)S(1)}, u32[]{:S(2)}, u32[]{:S(2)}) collective-permute-start(f32[128,1536]{1,0:T(8,128)S(1)} %get-tuple-element.17), channel_id=1, source_target_pairs={{0,2},{2,4},{4,6},{6,7},{7,5},{5,3},{3,1},{1,0},{8,10},{10,12},{12... | collective-permute-start | bytes 2359304 | tf_op jit(solution)/shard_map/ppermute | solution.py:214
  741.4 34.9 %collective-permute-start.42 = (f32[128,1536]{1,0:T(8,128)S(1)}, f32[128,1536]{1,0:T(8,128)S(1)}, u32[]{:S(2)}, u32[]{:S(2)}) collective-permute-start(f32[128,1536]{1,0:T(8,128)S(1)} %get-tuple-element.18), channel_id=1, source_target_pairs={{0,1},{2,0},{4,2},{6,4},{7,6},{5,7},{3,5},{1,3},{8,9},{10,8},{12,1... | collective-permute-start | bytes 2359304 | tf_op jit(solution)/shard_map/ppermute | solution.py:214
  757.1 86.0 %collective-permute-start.21 = (f32[128,1536]{1,0:T(8,128)S(1)}, f32[128,1536]{1,0:T(8,128)}, u32[]{:S(2)}, u32[]{:S(2)}) collective-permute-start(f32[128,1536]{1,0:T(8,128)S(1)} %get-tuple-element.33), channel_id=1, source_target_pairs={{0,2},{2,4},{4,6},{6,7},{7,5},{5,3},{3,1},{1,0},{8,10},{10,12},{12... | collective-permute-start | bytes 2359304 | tf_op jit(solution)/shard_map/ppermute | solution.py:214
  761.0 167.9 %collective-permute-start.60 = (f32[256,1536]{1,0:T(8,128)}, f32[256,1536]{1,0:T(8,128)}, u32[]{:S(2)}, u32[]{:S(2)}) collective-permute-start(f32[256,1536]{1,0:T(8,128)} %get-tuple-element.45), channel_id=1, source_target_pairs={{0,0},{1,1},{2,8},{3,9},{4,16},{5,17},{6,24},{7,25},{8,2},{9,3},{1... | collective-permute-start | bytes 4718600 | tf_op jit(solution)/shard_map/ppermute | solution.py:234
  774.3 154.6 %collective-permute-start.61 = (f32[256,1536]{1,0:T(8,128)}, f32[256,1536]{1,0:T(8,128)}, u32[]{:S(2)}, u32[]{:S(2)}) collective-permute-start(f32[256,1536]{1,0:T(8,128)} %get-tuple-element.46), channel_id=1, source_target_pairs={{0,1},{1,0},{2,9},{3,8},{4,17},{5,16},{6,25},{7,24},{8,3},{9,2},{1... | collective-permute-start | bytes 4718600 | tf_op jit(solution)/shard_map/ppermute | solution.py:234
  774.4 112.4 %collective-permute-start.28 = (f32[128,1536]{1,0:T(8,128)}, f32[128,1536]{1,0:T(8,128)}, u32[]{:S(2)}, u32[]{:S(2)}) collective-permute-start(f32[128,1536]{1,0:T(8,128)} %get-tuple-element.34), channel_id=1, source_target_pairs={{0,1},{2,0},{4,2},{6,4},{7,6},{5,7},{3,5},{1,3},{8,9},{10,8},{12,1... | collective-permute-start | bytes 2359304 | tf_op jit(solution)/shard_map/ppermute | solution.py:214
  779.1 147.7 %collective-permute-start.36 = (f32[128,1536]{1,0:T(8,128)}, f32[128,1536]{1,0:T(8,128)}, u32[]{:S(2)}, u32[]{:S(2)}) collective-permute-start(f32[128,1536]{1,0:T(8,128)} %get-tuple-element.15), channel_id=1, source_target_pairs={{0,2},{2,4},{4,6},{6,7},{7,5},{5,3},{3,1},{1,0},{8,10},{10,12},{12... | collective-permute-start | bytes 2359304 | tf_op jit(solution)/shard_map/ppermute | solution.py:214
  843.2 83.7 %collective-permute-start.43 = (f32[128,1536]{1,0:T(8,128)}, f32[128,1536]{1,0:T(8,128)}, u32[]{:S(2)}, u32[]{:S(2)}) collective-permute-start(f32[128,1536]{1,0:T(8,128)} %get-tuple-element.16), channel_id=1, source_target_pairs={{0,1},{2,0},{4,2},{6,4},{7,6},{5,7},{3,5},{1,3},{8,9},{10,8},{12,1... | collective-permute-start | bytes 2359304 | tf_op jit(solution)/shard_map/ppermute | solution.py:214
  888.8 53.8 %collective-permute-start.22 = (f32[128,1536]{1,0:T(8,128)S(1)}, f32[128,1536]{1,0:T(8,128)S(1)}, u32[]{:S(2)}, u32[]{:S(2)}) collective-permute-start(f32[128,1536]{1,0:T(8,128)S(1)} %get-tuple-element.31), channel_id=1, source_target_pairs={{0,2},{2,4},{4,6},{6,7},{7,5},{5,3},{3,1},{1,0},{8,10},{10,12},{12... | collective-permute-start | bytes 2359304 | tf_op jit(solution)/shard_map/ppermute | solution.py:214
  971.9 62.0 %collective-permute-start.45 = (f32[256,1536]{1,0:T(8,128)}, f32[256,1536]{1,0:T(8,128)}, u32[]{:S(2)}, u32[]{:S(2)}) collective-permute-start(f32[256,1536]{1,0:T(8,128)} %get-tuple-element.49), channel_id=1, source_target_pairs={{1,0},{0,1},{9,2},{8,3},{17,4},{16,5},{25,6},{24,7},{3,8},{2,9},{1... | collective-permute-start | bytes 4718600 | tf_op jit(solution)/shard_map/ppermute | solution.py:249
  1041.5 70.1 %collective-permute-start.76 = (f32[128,1536]{1,0:T(8,128)}, f32[128,1536]{1,0:T(8,128)S(1)}, u32[]{:S(2)}, u32[]{:S(2)}) collective-permute-start(f32[128,1536]{1,0:T(8,128)} %get-tuple-element.54), channel_id=1, source_target_pairs={{0,2},{2,4},{4,6},{6,7},{7,5},{5,3},{3,1},{1,0},{8,10},{10,12},{12... | collective-permute-start | bytes 2359304 | tf_op jit(solution)/shard_map/ppermute | solution.py:199
  1045.4 71.6 %collective-permute-start.77 = (f32[128,1536]{1,0:T(8,128)}, f32[128,1536]{1,0:T(8,128)S(1)}, u32[]{:S(2)}, u32[]{:S(2)}) collective-permute-start(f32[128,1536]{1,0:T(8,128)} %get-tuple-element.53), channel_id=1, source_target_pairs={{0,1},{2,0},{4,2},{6,4},{7,6},{5,7},{3,5},{1,3},{8,9},{10,8},{12,1... | collective-permute-start | bytes 2359304 | tf_op jit(solution)/shard_map/ppermute | solution.py:199
  1048.2 73.7 %collective-permute-start.62 = (f32[128,1536]{1,0:T(8,128)}, f32[128,1536]{1,0:T(8,128)S(1)}, u32[]{:S(2)}, u32[]{:S(2)}) collective-permute-start(f32[128,1536]{1,0:T(8,128)} %get-tuple-element.57), channel_id=1, source_target_pairs={{0,2},{2,4},{4,6},{6,7},{7,5},{5,3},{3,1},{1,0},{8,10},{10,12},{12... | collective-permute-start | bytes 2359304 | tf_op jit(solution)/shard_map/ppermute | solution.py:199
  1166.5 33.8 %collective-permute-start.67 = (f32[128,1536]{1,0:T(8,128)S(1)}, f32[128,1536]{1,0:T(8,128)S(1)}, u32[]{:S(2)}, u32[]{:S(2)}) collective-permute-start(f32[128,1536]{1,0:T(8,128)S(1)} %collective-permute-done.65), channel_id=1, source_target_pairs={{0,1},{2,0},{4,2},{6,4},{7,6},{5,7},{3,5},{1,3},{8,9},{10,8},{12,1... | collective-permute-start | bytes 2359304 | tf_op jit(solution)/shard_map/ppermute | solution.py:199
  1188.3 33.8 %collective-permute-start.68 = (f32[128,1536]{1,0:T(8,128)S(1)}, f32[128,1536]{1,0:T(8,128)S(1)}, u32[]{:S(2)}, u32[]{:S(2)}) collective-permute-start(f32[128,1536]{1,0:T(8,128)S(1)} %collective-permute-done.66), channel_id=1, source_target_pairs={{0,2},{2,4},{4,6},{6,7},{7,5},{5,3},{3,1},{1,0},{8,10},{10,12},{12... | collective-permute-start | bytes 2359304 | tf_op jit(solution)/shard_map/ppermute | solution.py:199
  1217.1 33.7 %collective-permute-start.85 = (f32[128,1536]{1,0:T(8,128)S(1)}, f32[128,1536]{1,0:T(8,128)S(1)}, u32[]{:S(2)}, u32[]{:S(2)}) collective-permute-start(f32[128,1536]{1,0:T(8,128)S(1)} %collective-permute-done.83), channel_id=1, source_target_pairs={{0,1},{2,0},{4,2},{6,4},{7,6},{5,7},{3,5},{1,3},{8,9},{10,8},{12,1... | collective-permute-start | bytes 2359304 | tf_op jit(solution)/shard_map/ppermute | solution.py:199
  1250.8 33.9 %collective-permute-start.87 = (f32[128,1536]{1,0:T(8,128)S(1)}, f32[128,1536]{1,0:T(8,128)S(1)}, u32[]{:S(2)}, u32[]{:S(2)}) collective-permute-start(f32[128,1536]{1,0:T(8,128)S(1)} %collective-permute-done.85), channel_id=1, source_target_pairs={{0,1},{2,0},{4,2},{6,4},{7,6},{5,7},{3,5},{1,3},{8,9},{10,8},{12,1... | collective-permute-start | bytes 2359304 | tf_op jit(solution)/shard_map/ppermute | solution.py:199
  1255.8 33.9 %collective-permute-start.72 = (f32[128,1536]{1,0:T(8,128)S(1)}, f32[128,1536]{1,0:T(8,128)S(1)}, u32[]{:S(2)}, u32[]{:S(2)}) collective-permute-start(f32[128,1536]{1,0:T(8,128)S(1)} %collective-permute-done.70), channel_id=1, source_target_pairs={{0,2},{2,4},{4,6},{6,7},{7,5},{5,3},{3,1},{1,0},{8,10},{10,12},{12... | collective-permute-start | bytes 2359304 | tf_op jit(solution)/shard_map/ppermute | solution.py:199
  (70 other events, 2434.4 us)
Sparse Core Ops, SparseCore 0:
  10.7 140.2 all-gather.2
  433.7 38.6 reduce-scatter.4
  474.9 37.9 reduce-scatter.6
  515.2 37.8 reduce-scatter.8
  555.5 37.9 reduce-scatter.10
  1039.0 151.8 all-gather.4
